TPU v7x, 128 devices: a whole 4x4x4 slice. The times are simulated.
128 devices in a mesh: gx: 16 (over x, y), gy: 4 (over z), gz: 2 (over core).
Axes of the slice: x: 4, y: 4, z: 4, core: 2. Of those that a mesh axis runs over, the one named last changes fastest.
Arguments:
- conserved: float32 [14, 128, 256, 512], P(None, 'gx', 'gy', 'gz')
- char_left: float32 [14, 14], replicated
- char_right: float32 [14, 14], replicated
- shock_list: int32 [16, 4, 2, 128], P('gx', 'gy', 'gz'), may hold values from 0 to 511, as said below
- shock_count: int32 [16, 4, 2], P('gx', 'gy', 'gz'), may hold values from 32 to 128, as said below
Outputs:
- advanced: float32 [14, 128, 256, 512], P(None, 'gx', 'gy', 'gz')
Inputs may be any that keep to these rules, and one draw needn't show every extreme that they name: `shock_list`: the entries of one device's list are distinct local pencil indices; only the first shock_count of them are shocked pencils. `shock_count`: in every column of devices along gx (fixed gy and gz index) one device has 128 shocked pencils and every other device has 32, so a column holds 608 in all.
All inputs are finite; a program needn't handle non-finite values.
Results may differ from a plain program's by a relative error of at most 0.00005.
Values sent between devices are 32-bit elements; how exact they have to be, the bound alone decides.
A program may use at most 192 MiB of HBM per device.

v0:
```python
import functools

import jax
import jax.numpy as jnp
import numpy as np
from jax import lax
from jax.experimental import pallas as pl
from jax.experimental.pallas import tpu as pltpu
from jax.sharding import PartitionSpec as P

SPECIES = 9
VARIABLES = 14
CX, CY, CZ = 8, 64, 256
ROWS = CX * CY
PENCILS = 128
GROUP = 16
SIZE = VARIABLES * GROUP
CELLS = 280
TILES = 33
EPS = 0.5e-6
SCALE = 0.2 / 60.0

F32 = jnp.float32
BF16 = jnp.bfloat16
VMEM = pl.BlockSpec(memory_space=pltpu.VMEM)
SMEM = pl.BlockSpec(memory_space=pltpu.SMEM)
HBM = pl.BlockSpec(memory_space=pltpu.HBM)


def lanes(shape):
    return lax.broadcasted_iota(jnp.int32, shape, len(shape) - 1)


def split(values):
    high = values.astype(BF16)
    low = (values - high.astype(F32)).astype(BF16)
    return high, low


def dot(left, right):
    return jnp.dot(left, right, preferred_element_type=F32)


def state_of(read):
    density = read(0)
    for v in range(1, SPECIES):
        density = density + read(v)
    inverse = 1.0 / density
    m0, m1, m2 = read(9), read(10), read(11)
    squares = m0 * m0 + m1 * m1 + m2 * m2
    pressure = 0.4 * (read(12) - read(13) - 0.5 * squares * inverse)
    return m1 * inverse, m2 * inverse, pressure


def flux(value, velocity, pressure, scaled_pressure, v, normal):
    if v == SPECIES + 3:
        return (value + pressure) * velocity
    if v == SPECIES + normal:
        return value * velocity + scaled_pressure
    return value * velocity


def scaled(state):
    velocity1, velocity2, pressure = state
    return SCALE * velocity1, SCALE * velocity2, pressure, SCALE * pressure


def expand(matrix, scale, target):
    row = lax.broadcasted_iota(jnp.int32, (SIZE, SIZE), 0)
    column = lax.broadcasted_iota(jnp.int32, (SIZE, SIZE), 1)
    same = (row & (GROUP - 1)) == (column & (GROUP - 1))
    spread = (
        lax.broadcasted_iota(jnp.int32, (SIZE, VARIABLES), 0) // GROUP
        == lax.broadcasted_iota(jnp.int32, (SIZE, VARIABLES), 1)
    ).astype(BF16)
    gather = (
        lax.broadcasted_iota(jnp.int32, (VARIABLES, SIZE), 1) // GROUP
        == lax.broadcasted_iota(jnp.int32, (VARIABLES, SIZE), 0)
    ).astype(BF16)
    for part, places in zip(split(scale * matrix), ((0, 1), (2,))):
        wide = dot(spread, dot(part, gather).astype(BF16))
        wide = jnp.where(same, wide, 0.0).astype(BF16)
        for place in places:
            target[:, SIZE * place : SIZE * place + SIZE] = wide


def project(matrix, values):
    high, low = split(values)
    return dot(matrix[...], jnp.concatenate([high, low, high], axis=0))


def face_sums(speed, pull_ref, proj, velocity_ref, pressure_ref, scratch, sums):
    fast_ref, slow_ref, plus_ref, minus_ref, terms = scratch

    def sides(i, carry):
        rows = pl.ds(pl.multiple_of(8 * i, 8), 8)
        fast_ref[rows, :] = velocity_ref[rows, :] + speed
        slow_ref[rows, :] = velocity_ref[rows, :] - speed
        return carry

    lax.fori_loop(0, 34, sides, 0, unroll=2)

    def component(v, carry):
        pull = jnp.broadcast_to(pull_ref[0, pl.ds(v, 1), :], (8, 128))
        push = jnp.broadcast_to(pull_ref[1, pl.ds(v, 1), :], (8, 128))

        def fluxes(i, carry):
            rows = pl.ds(pl.multiple_of(8 * i, 8), 8)
            velocity = velocity_ref[rows, :]
            base = proj[v, rows, :]
            source = pressure_ref[rows, :] * (pull + velocity * push)
            plus_ref[rows, :] = fast_ref[rows, :] * base + source
            minus_ref[rows, :] = slow_ref[rows, :] * base + source
            return carry

        lax.fori_loop(0, 34, fluxes, 0, unroll=34)

        def pairs(i, carry):
            row = pl.multiple_of(8 * i, 8)
            for side, source in enumerate((plus_ref, minus_ref)):
                middle = source[pl.ds(row + 6, 8), :]
                x = middle - source[pl.ds(row + 5, 8), :]
                y = source[pl.ds(row + 7, 8), :] - middle
                xx, xy, yy = x * x, x * y, y * y
                shared = (xx + yy) * (2.0 / 3.0) + (EPS - xy * (11.0 / 6.0))
                lean, even, back = 1.0 / (shared + yy), 1.0 / (shared + xy), 1.0 / (shared + xx)
                x2, y2 = x + x, y + y
                if side == 0:
                    w0, w1, w2 = lean * lean, 6.0 * (even * even), 3.0 * (back * back)
                    n0, n1, n2 = 5.0 * y - x2, x + y2, (x2 + x2) - y
                else:
                    w0, w1, w2 = back * back, 6.0 * (even * even), 3.0 * (lean * lean)
                    n0, n1, n2 = 5.0 * x - y2, y + x2, (y2 + y2) - x
                for k, value in enumerate((w0, w1, w2, w0 * n0, w1 * n1, w2 * n2)):
                    terms[6 * side + k, pl.ds(row, 8), :] = value
            return carry

        lax.fori_loop(0, TILES, pairs, 0, unroll=33)

        def faces(i, carry):
            row = pl.multiple_of(8 * i, 8)

            def at(k, by):
                return terms[k, pl.ds(row + by, 8), :]

            gain = (at(3, 0) + at(4, 1) + at(5, 2)) / (at(0, 0) + at(1, 1) + at(2, 2))
            loss = (at(9, 3) + at(10, 2) + at(11, 1)) / (at(6, 3) + at(7, 2) + at(8, 1))
            base = plus_ref[pl.ds(row + 7, 8), :] + minus_ref[pl.ds(row + 8, 8), :]
            sums[v, pl.ds(row, 8), :] = base + (gain - loss) * (1.0 / 6.0)
            return carry

        lax.fori_loop(0, TILES, faces, 0, unroll=33)
        return carry

    lax.fori_loop(0, VARIABLES, component, 0)


def prepare_body(
    list_ref, where_ref, left_ref, right_ref, u_hbm,
    u_ref, sums, yflux, zflux, kr_out,
    proj, velocity_ref, pressure_ref, pull_ref,
    rows_ref, cells, kl_ref, up_send, down_send, z_send, y_recv, z_recv,
    load_sems, send_sems, recv_sems, *scratch,
):
    loads = []

    def load(index, t, x, y):
        copy = pltpu.make_async_copy(
            u_hbm.at[:, x, y, pl.ds(128 * t, 128)], u_ref.at[t, :, x, y], load_sems.at[index]
        )
        copy.start()
        loads.append(copy)

    every = pl.ds(0, CX)
    for t in range(2):
        load(len(loads), t, every, pl.ds(0, 8))
        load(len(loads), t, every, pl.ds(CY - 8, 8))
    gy, gz = lax.axis_index("gy"), lax.axis_index("gz")
    ny = lax.axis_size("gy")
    above, below = {"gy": lax.rem(gy + 1, ny)}, {"gy": lax.rem(gy + ny - 1, ny)}
    beside = {"gz": 1 - gz}
    barrier = pltpu.get_barrier_semaphore()
    for device in (above, below, beside):
        pl.semaphore_signal(barrier, inc=1, device_id=device, device_id_type=pl.DeviceIdType.MESH)

    def remote(index, source, target, device):
        return pltpu.make_async_remote_copy(
            src_ref=source,
            dst_ref=target,
            send_sem=send_sems.at[index],
            recv_sem=recv_sems.at[index],
            device_id=device,
            device_id_type=pl.DeviceIdType.MESH,
        )

    for x in range(2):
        for t in range(2):
            load(len(loads), t, pl.ds(x, 1), pl.ds(8, CY - 16))
    for copy in loads[:4]:
        copy.wait()
    for x in range(2, CX):
        for t in range(2):
            load(len(loads), t, pl.ds(x, 1), pl.ds(8, CY - 16))

    def y_ends(v, carry):
        for t in range(2):
            for x in range(CX):
                down_send[t, v, 3 * x : 3 * x + 3, :] = u_ref[t, v, x, 0:3, :]
                up_send[t, v, 3 * x : 3 * x + 3, :] = u_ref[t, v, x, CY - 3 : CY, :]
        return carry

    lax.fori_loop(0, VARIABLES, y_ends, 0)
    expand(left_ref[...], 0.5, kl_ref)
    for k in range(2):
        at = SPECIES + 2 + k
        pull_ref[k, 0:VARIABLES, :] = jnp.broadcast_to(
            0.5 * left_ref[:, at : at + 1], (VARIABLES, 128)
        )
    pl.semaphore_wait(barrier, 3)
    up = remote(0, up_send, y_recv.at[0], above)
    down = remote(1, down_send, y_recv.at[1], below)
    up.start()
    down.start()
    expand(right_ref[...], 0.2, kr_out)

    lane = lanes((CY, 128))
    source = lax.broadcasted_iota(jnp.int32, (CX * 128, 128), 0)
    place = lax.broadcasted_iota(jnp.int32, (CX * 128, 128), 1)
    within = ((source & 127) + 3) & 127
    wanted = jnp.minimum(place & 15, 5)
    select = ((place // 16 == source // 128) & (within == wanted)).astype(BF16)
    width = 128 * CX
    for part in range(2):
        some = range(part * CX // 2, (part + 1) * CX // 2)
        for copy in loads[4 + part * CX : 4 + (part + 1) * CX]:
            copy.wait()
        chosen = select[part * width // 2 : (part + 1) * width // 2]
        chosen = jnp.concatenate([chosen, chosen], axis=0)

        def z_ends(v, carry, part=part, some=some, chosen=chosen):
            highs, lows = [], []
            for x in some:
                high, low = split(jnp.where(lane < 64, u_ref[0, v, x], u_ref[1, v, x]))
                highs.append(high)
                lows.append(low)
            packed = dot(jnp.concatenate(highs + lows, axis=1), chosen)
            z_send[v] = packed if part == 0 else z_send[v] + packed
            return carry

        lax.fori_loop(0, VARIABLES, z_ends, 0, unroll=7)

    flat = u_ref.reshape(2, VARIABLES * ROWS, 128)
    packed = rows_ref.reshape(2, VARIABLES * PENCILS, 128)

    def gather(p, carry):
        row = list_ref[p]
        for t in range(2):
            for v in range(VARIABLES):
                packed[t, pl.ds(p + v * PENCILS, 1), :] = flat[t, pl.ds(row + v * ROWS, 1), :]
        return carry

    lax.fori_loop(0, 8, gather, 0, unroll=2)
    ends = remote(2, z_send, z_recv, beside)
    ends.start()
    lax.fori_loop(8, PENCILS, gather, 0, unroll=2)

    def turn(v, carry):
        for t in range(2):
            cells[v, 8 + 128 * t : 136 + 128 * t, :] = rows_ref[t, v].T
        return carry

    lax.fori_loop(0, VARIABLES, turn, 0, unroll=7)

    def wave(i, peak):
        rows = pl.ds(pl.multiple_of(8 * i, 8), 8)
        _, velocity, pressure = state_of(lambda v: cells[v, rows, :])
        velocity_ref[rows, :] = velocity
        pressure_ref[rows, :] = pressure
        return jnp.maximum(peak, jnp.abs(velocity))

    peak = lax.fori_loop(1, 33, wave, jnp.zeros((8, 128), F32), unroll=2)

    def chunk(i, carry):
        first = pl.ds(pl.multiple_of(32 * i + 8, 8), 16)
        second = pl.ds(pl.multiple_of(32 * i + 24, 8), 16)
        values = jnp.concatenate([cells[:, first, :], cells[:, second, :]], axis=-1)
        result = project(kl_ref, values.reshape(SIZE, 256))
        proj[:, first, :] = result[:, 0:128].reshape(VARIABLES, 16, 128)
        proj[:, second, :] = result[:, 128:256].reshape(VARIABLES, 16, 128)
        return carry

    lax.fori_loop(0, CZ // 32, chunk, 0, unroll=4)

    ends.wait()
    own_y = jnp.broadcast_to(where_ref[...] % CY, (2 * CY, PENCILS))
    pick = own_y == lax.broadcasted_iota(jnp.int32, (2 * CY, PENCILS), 0) % CY
    pick = pick.astype(BF16)
    own_x = jnp.broadcast_to(where_ref[...] // CY, (16, 128))

    def turn_ends(v, carry):
        values = z_recv[v]
        high = values.astype(BF16).astype(F32)
        both = jnp.concatenate([high, values - high], axis=0).T
        turned = dot(both.astype(BF16), pick)
        near = turned[0:16]
        for x in range(1, CX):
            near = jnp.where(own_x == x, turned[16 * x : 16 * x + 16], near)
        cells[v, 0:5, :] = near[0:5]
        cells[v, 5:8, :] = near[0:3]
        cells[v, 264:267, :] = near[3:6]
        cells[v, 267:272, :] = near[0:5]
        return carry

    lax.fori_loop(0, VARIABLES, turn_ends, 0, unroll=7)
    peak = wave(0, peak)
    peak = wave(33, peak)
    speed = jnp.broadcast_to(jnp.max(peak, axis=0, keepdims=True) + 1.0, (8, 128))
    values = jnp.concatenate([cells[:, 0:8, :], cells[:, 264:272, :]], axis=1)
    result = project(kl_ref, values.reshape(SIZE, 128)).reshape(VARIABLES, 16, 128)
    proj[:, 0:8, :] = result[:, 0:8]
    proj[:, 264:272, :] = result[:, 8:16]

    _, velocity, pressure, scaled_pressure = scaled(state_of(lambda v: z_recv[v]))
    for v in range(VARIABLES):
        high, low = split(flux(z_recv[v], velocity, pressure, scaled_pressure, v, 2))
        zflux[v, :, 0:128] = high
        zflux[v, :, 128:256] = low

    face_sums(speed, pull_ref, proj, velocity_ref, pressure_ref, scratch, sums)

    up.wait()
    down.wait()
    for side in range(2):
        for t in range(2):
            state = scaled(state_of(lambda v: y_recv[side, t, v]))
            for v in range(VARIABLES):
                yflux[side, t, v] = flux(y_recv[side, t, v], state[0], state[2], state[3], v, 1)


def prepare(shocked, left, right, conserved):
    return pl.pallas_call(
        prepare_body,
        out_shape=(
            pltpu.VMEM((2, VARIABLES, CX, CY, 128), F32),
            pltpu.VMEM((VARIABLES, CELLS, 128), F32),
            pltpu.VMEM((2, 2, VARIABLES, 3 * CX, 128), F32),
            pltpu.VMEM((VARIABLES, CY, 256), BF16),
            pltpu.VMEM((SIZE, 3 * SIZE), BF16),
        ),
        in_specs=[SMEM, VMEM, VMEM, VMEM, HBM],
        out_specs=(VMEM,) * 5,
        scratch_shapes=[
            pltpu.VMEM((VARIABLES, CELLS, 128), F32),
            pltpu.VMEM((CELLS, 128), F32),
            pltpu.VMEM((CELLS, 128), F32),
            pltpu.VMEM((2, 16, 128), F32),
            pltpu.VMEM((2, VARIABLES, PENCILS, 128), F32),
            pltpu.VMEM((VARIABLES, 272, 128), F32),
            pltpu.VMEM((SIZE, 3 * SIZE), BF16),
            pltpu.VMEM((2, VARIABLES, 3 * CX, 128), F32),
            pltpu.VMEM((2, VARIABLES, 3 * CX, 128), F32),
            pltpu.VMEM((VARIABLES, CY, 128), F32),
            pltpu.VMEM((2, 2, VARIABLES, 3 * CX, 128), F32),
            pltpu.VMEM((VARIABLES, CY, 128), F32),
            pltpu.SemaphoreType.DMA((4 + 2 * CX,)),
            pltpu.SemaphoreType.DMA((3,)),
            pltpu.SemaphoreType.DMA((3,)),
            pltpu.VMEM((CELLS, 128), F32),
            pltpu.VMEM((CELLS, 128), F32),
            pltpu.VMEM((CELLS, 128), F32),
            pltpu.VMEM((CELLS, 128), F32),
            pltpu.VMEM((12, CELLS, 128), F32),
        ],
        compiler_params=pltpu.CompilerParams(
            collective_id=0, has_side_effects=True, vmem_limit_bytes=46 << 20
        ),
        name="prepare",
    )(shocked, shocked.reshape(1, PENCILS), left, right, conserved)


def weno_terms(sums, kr_ref, across, terms_out):
    def chunk(i, carry):
        start = pl.multiple_of(32 * i, 8)

        def change(by):
            return sums[:, pl.ds(start + by + 1, 16), :] - sums[:, pl.ds(start + by, 16), :]

        values = jnp.concatenate([change(0), change(16)], axis=-1)
        result = project(kr_ref, values.reshape(SIZE, 256))
        for k in range(2):
            rows = pl.ds(pl.multiple_of(start + 16 * k, 8), 16)
            across[:, rows, :] = result[:, 128 * k : 128 * k + 128].reshape(VARIABLES, 16, 128)
        return carry

    lax.fori_loop(0, CZ // 32, chunk, 0, unroll=4)

    def turn_back(v, carry):
        for t in range(2):
            terms_out[t, v] = across[v, 128 * t : 128 * t + 128, :].T
        return carry

    lax.fori_loop(0, VARIABLES, turn_back, 0, unroll=2)


def advance_body(
    list_ref, count_ref, u_ref,
    sums, yflux, zflux, kr_ref, zcoef_ref, hcoef_ref,
    out_ref,
    hx_ref, replaced, mask_ref, v1_ref, p_ref, stage, along_z, along_y, across, terms_out,
):
    x = pl.program_id(0)

    @pl.when(x == 0)
    def _():
        weno_terms(sums, kr_ref, across, terms_out)
        hx_ref[...] = jnp.zeros((256, CZ), BF16)
        mask_ref[...] = jnp.zeros((ROWS, 128), F32)
        flat = replaced.reshape(2, VARIABLES * ROWS, 128)
        packed = terms_out.reshape(2, VARIABLES * PENCILS, 128)

        def scatter(p, carry):
            row = list_ref[p]
            mask_ref[pl.ds(row, 1), :] = jnp.ones((1, 128), F32)
            for t in range(2):
                for v in range(VARIABLES):
                    flat[t, pl.ds(row + v * ROWS, 1), :] = packed[t, pl.ds(p + v * PENCILS, 1), :]
            return carry

        lax.fori_loop(0, count_ref[0, 0, 0], scatter, 0)

    @pl.when(x > 0)
    def _():
        for part in range(2):
            old = pl.ds(pl.multiple_of(128 * part + 16 * x - 16, 16), 16)
            hx_ref[old, :] = jnp.zeros((16, CZ), BF16)

    for part in range(2):
        new = pl.ds(pl.multiple_of(128 * part + 16 * x, 16), 16)
        hx_ref[new, :] = hcoef_ref[...]

    for t in range(2):
        cut = slice(128 * t, 128 * t + 128)
        velocity1, velocity2, pressure, scaled_pressure = scaled(
            state_of(lambda v: u_ref[t, v, x])
        )
        v1_ref[t] = velocity1
        p_ref[0, t] = pressure
        p_ref[1, t] = scaled_pressure
        for v in range(VARIABLES):
            high, low = split(flux(u_ref[t, v, x], velocity2, pressure, scaled_pressure, v, 2))
            stage[v, :, cut] = high
            stage[v, :, 256 + 128 * t : 384 + 128 * t] = low

    rows = VARIABLES * CY
    along_z[...] = dot(
        jnp.concatenate([stage[...].reshape(rows, 512), zflux[...].reshape(rows, 256)], axis=1),
        jnp.concatenate([zcoef_ref[...], zcoef_ref[...], hx_ref[...]], axis=0),
    ).reshape(VARIABLES, CY, CZ)

    hit = mask_ref[pl.ds(pl.multiple_of(CY * x, CY), CY), :] > 0.5
    for v in range(VARIABLES):
        for t in range(2):
            cut = slice(128 * t, 128 * t + 128)
            buffer = along_y.at[v % 2, t]
            value = u_ref[t, v, x]
            buffer[5:8, :] = yflux[0, t, v, pl.ds(3 * x, 3), :]
            buffer[8:72, :] = flux(value, v1_ref[t], p_ref[0, t], p_ref[1, t], v, 1)
            buffer[72:75, :] = yflux[1, t, v, pl.ds(3 * x, 3), :]

            def at(by):
                return buffer[8 + by : 72 + by, :]

            y_term = 45.0 * (at(1) - at(-1)) - 9.0 * (at(2) - at(-2)) + (at(3) - at(-3))
            z_term = jnp.where(hit, replaced[t, v, x], along_z[v, :, cut])
            out_ref[v, 0, :, cut] = value - (y_term + z_term)


def advance(shocked, live_count, prepared, coefs):
    return pl.pallas_call(
        advance_body,
        grid=(CX,),
        out_shape=jax.ShapeDtypeStruct((VARIABLES, CX, CY, CZ), F32),
        in_specs=[SMEM, SMEM] + [VMEM] * 7,
        out_specs=pl.BlockSpec((VARIABLES, 1, CY, CZ), lambda x: (0, x, 0, 0)),
        scratch_shapes=[
            pltpu.VMEM((256, CZ), BF16),
            pltpu.VMEM((2, VARIABLES, CX, CY, 128), F32),
            pltpu.VMEM((ROWS, 128), F32),
            pltpu.VMEM((2, CY, 128), F32),
            pltpu.VMEM((2, 2, CY, 128), F32),
            pltpu.VMEM((VARIABLES, CY, 512), BF16),
            pltpu.VMEM((VARIABLES, CY, CZ), F32),
            pltpu.VMEM((2, 2, 80, 128), F32),
            pltpu.VMEM((VARIABLES, CZ, 128), F32),
            pltpu.VMEM((2, VARIABLES, PENCILS, 128), F32),
        ],
        compiler_params=pltpu.CompilerParams(vmem_limit_bytes=36 << 20),
        name="advance",
    )(shocked, live_count, *prepared, *coefs)


@functools.cache
def coefficients():
    weight = {1: 45.0, -1: -45.0, 2: -9.0, -2: 9.0, 3: 1.0, -3: -1.0}

    def coef(offset):
        return weight.get(offset, 0.0)

    zcoef = np.array([[coef(c - k) for k in range(CZ)] for c in range(CZ)])
    cells = [-3, -2, -1, CZ, CZ + 1, CZ + 2]
    hcoef = np.zeros((16, CZ))
    for j, c in enumerate(cells):
        for k in range(CZ):
            hcoef[j, k] = coef(c - k)
    return zcoef, hcoef


def on_device(conserved, char_left, char_right, shock_list, shock_count):
    shocked = shock_list.reshape(PENCILS)
    prepared = prepare(shocked, char_left, char_right, conserved)
    coefs = [jnp.asarray(m, BF16) for m in coefficients()]
    return advance(shocked, shock_count, prepared, coefs)


def solution(mesh):
    placed = (P(None, "gx", "gy", "gz"), P(), P(), P("gx", "gy", "gz", None), P("gx", "gy", "gz"))
    return jax.shard_map(
        on_device, mesh=mesh, in_specs=placed, out_specs=P(None, "gx", "gy", "gz"), check_vma=False
    )
```

profile of v0, /device:TPU:30, one launch (start us, length us, event | category | flops | bytes accessed | tf_op | source)
XLA Modules:
  0.0 33.4 jit_solution(15746482396464634805)
XLA Ops:
  0.0 0.0 copy-start.1
  0.0 0.0 copy-start
  0.0 0.0 copy-start.2
  0.7 18.4 %prepare.1 = (f32[2,14,8,64,128]{4,3,2,1,0:T(8,128)S(1)}, f32[14,280,128]{2,1,0:T(8,128)S(1)}, f32[2,2,14,24,128]{4,3,2,1,0:T(8,128)S(1)}, bf16[14,64,256]{2,1,0:T(8,128)(2,1)S(1)}, bf16[224,672]{1,0:T(8,128)(2,1)S(1)}) custom-call(s32[128]{0:T(128)} %bitcast.2, s32[1,128]{1,0:T(1,128)} %bitcast.3, f32[14,14]{1,0:T(8,128)} %left_ref.1, f32[14,14]{1,0:T(8,128)} %right_ref.1, ...), custom_call_target="tpu_custom_call" | custom-call | tf_op jit(solution)/shard_map/prepare/pallas_call | solution.py:341
  19.1 0.0 copy-done.1
  19.1 0.0 copy-done
  19.2 0.0 copy-done.2
  19.2 14.2 %advance.1 = f32[14,8,64,256]{3,2,1,0:T(8,128)} custom-call(s32[128]{0:T(128)S(1)} %bitcast.4, s32[1,1,1]{2,1,0:T(1,128)S(6)} %copy.8.count_ref, f32[2,14,8,64,128]{4,3,2,1,0:T(8,128)S(1)} %get-tuple-element.10.u_ref, f32[14,280,128]{2,1,0:T(8,128)S(1)} %get-tuple-element.11.sums, f32[2,2,14,24,128]{4,3,2,1,0:T(8,128)S(1)} %get-tuple-element.12.yflux, ...), custom_call_target="tpu_custom_call" | custom-call | tf_op jit(solution)/shard_map/advance/pallas_call | solution.py:479
Async XLA Ops:
  0.0 19.1 %copy-start.1 = (bf16[16,256]{1,0:T(8,128)(2,1)S(1)}, bf16[16,256]{1,0:T(8,128)(2,1)}, u32[]{:S(2)}) copy-start(bf16[16,256]{1,0:T(8,128)(2,1)} %constant.5.clone.hcoef_ref) | copy-start | bytes 24580
  0.0 19.1 %copy-start = (bf16[256,256]{1,0:T(8,128)(2,1)S(1)}, bf16[256,256]{1,0:T(8,128)(2,1)}, u32[]{:S(2)}) copy-start(bf16[256,256]{1,0:T(8,128)(2,1)} %constant.4.clone.zcoef_ref) | copy-start | bytes 393220
  0.0 19.2 %copy-start.2 = (s32[1,1,1,128]{3,2,1,0:T(1,128)S(1)}, s32[1,1,1,128]{3,2,1,0:T(1,128)}, u32[]{:S(2)}) copy-start(s32[1,1,1,128]{3,2,1,0:T(1,128)} %param.10) | copy-start | bytes 1540
where the time goes:
time: 33.6 us; the launch traced here: 33.4 us
  Pallas kernels  32.7 us (97%)
  between operations  0.72 us (2%)
    pallas_call x1, Pallas kernels, prepare(): pl.pallas_call(prepare_body, out_shape=(pltpu.VMEM((2, VARIABLES, CX, CY,...  18.4 us
    pallas_call x1, Pallas kernels, advance(): pl.pallas_call(advance_body, grid=(CX,), out_shape=jax.ShapeDtypeStruct((...  14.2 us

commit v1 on v0

--- a/solution.py
+++ b/solution.py
@@ -155,10 +155,34 @@
     lax.fori_loop(0, VARIABLES, component, 0)
 
 
+def weno_terms(sums, kr_ref, across, terms_out):
+    def chunk(i, carry):
+        start = pl.multiple_of(32 * i, 8)
+
+        def change(by):
+            return sums[:, pl.ds(start + by + 1, 16), :] - sums[:, pl.ds(start + by, 16), :]
+
+        values = jnp.concatenate([change(0), change(16)], axis=-1)
+        result = project(kr_ref, values.reshape(SIZE, 256))
+        for k in range(2):
+            rows = pl.ds(pl.multiple_of(start + 16 * k, 8), 16)
+            across[:, rows, :] = result[:, 128 * k : 128 * k + 128].reshape(VARIABLES, 16, 128)
+        return carry
+
+    lax.fori_loop(0, CZ // 32, chunk, 0, unroll=4)
+
+    def turn_back(v, carry):
+        for t in range(2):
+            terms_out[t, v] = across[v, 128 * t : 128 * t + 128, :].T
+        return carry
+
+    lax.fori_loop(0, VARIABLES, turn_back, 0, unroll=2)
+
+
 def prepare_body(
     list_ref, where_ref, left_ref, right_ref, u_hbm,
-    u_ref, sums, yflux, zflux, kr_out,
-    proj, velocity_ref, pressure_ref, pull_ref,
+    u_ref, terms_out, yflux, zflux,
+    sums, across, kr_out, proj, velocity_ref, pressure_ref, pull_ref,
     rows_ref, cells, kl_ref, up_send, down_send, z_send, y_recv, z_recv,
     load_sems, send_sems, recv_sems, *scratch,
 ):
@@ -216,11 +240,6 @@
         pull_ref[k, 0:VARIABLES, :] = jnp.broadcast_to(
             0.5 * left_ref[:, at : at + 1], (VARIABLES, 128)
         )
-    pl.semaphore_wait(barrier, 3)
-    up = remote(0, up_send, y_recv.at[0], above)
-    down = remote(1, down_send, y_recv.at[1], below)
-    up.start()
-    down.start()
     expand(right_ref[...], 0.2, kr_out)
 
     lane = lanes((CY, 128))
@@ -248,6 +267,12 @@
             return carry
 
         lax.fori_loop(0, VARIABLES, z_ends, 0, unroll=7)
+        if part == 0:
+            pl.semaphore_wait(barrier, 3)
+            up = remote(0, up_send, y_recv.at[0], above)
+            down = remote(1, down_send, y_recv.at[1], below)
+            up.start()
+            down.start()
 
     flat = u_ref.reshape(2, VARIABLES * ROWS, 128)
     packed = rows_ref.reshape(2, VARIABLES * PENCILS, 128)
@@ -327,6 +352,7 @@
         zflux[v, :, 128:256] = low
 
     face_sums(speed, pull_ref, proj, velocity_ref, pressure_ref, scratch, sums)
+    weno_terms(sums, kr_out, across, terms_out)
 
     up.wait()
     down.wait()
@@ -342,14 +368,16 @@
         prepare_body,
         out_shape=(
             pltpu.VMEM((2, VARIABLES, CX, CY, 128), F32),
-            pltpu.VMEM((VARIABLES, CELLS, 128), F32),
+            pltpu.VMEM((2, VARIABLES, PENCILS, 128), F32),
             pltpu.VMEM((2, 2, VARIABLES, 3 * CX, 128), F32),
             pltpu.VMEM((VARIABLES, CY, 256), BF16),
-            pltpu.VMEM((SIZE, 3 * SIZE), BF16),
         ),
         in_specs=[SMEM, VMEM, VMEM, VMEM, HBM],
-        out_specs=(VMEM,) * 5,
+        out_specs=(VMEM,) * 4,
         scratch_shapes=[
+            pltpu.VMEM((VARIABLES, CELLS, 128), F32),
+            pltpu.VMEM((VARIABLES, CZ, 128), F32),
+            pltpu.VMEM((SIZE, 3 * SIZE), BF16),
             pltpu.VMEM((VARIABLES, CELLS, 128), F32),
             pltpu.VMEM((CELLS, 128), F32),
             pltpu.VMEM((CELLS, 128), F32),
@@ -378,45 +406,20 @@
     )(shocked, shocked.reshape(1, PENCILS), left, right, conserved)
 
 
-def weno_terms(sums, kr_ref, across, terms_out):
-    def chunk(i, carry):
-        start = pl.multiple_of(32 * i, 8)
-
-        def change(by):
-            return sums[:, pl.ds(start + by + 1, 16), :] - sums[:, pl.ds(start + by, 16), :]
-
-        values = jnp.concatenate([change(0), change(16)], axis=-1)
-        result = project(kr_ref, values.reshape(SIZE, 256))
-        for k in range(2):
-            rows = pl.ds(pl.multiple_of(start + 16 * k, 8), 16)
-            across[:, rows, :] = result[:, 128 * k : 128 * k + 128].reshape(VARIABLES, 16, 128)
-        return carry
-
-    lax.fori_loop(0, CZ // 32, chunk, 0, unroll=4)
-
-    def turn_back(v, carry):
-        for t in range(2):
-            terms_out[t, v] = across[v, 128 * t : 128 * t + 128, :].T
-        return carry
-
-    lax.fori_loop(0, VARIABLES, turn_back, 0, unroll=2)
-
-
 def advance_body(
     list_ref, count_ref, u_ref,
-    sums, yflux, zflux, kr_ref, zcoef_ref, hcoef_ref,
+    terms_ref, yflux, zflux, zcoef_ref, hcoef_ref,
     out_ref,
-    hx_ref, replaced, mask_ref, v1_ref, p_ref, stage, along_z, along_y, across, terms_out,
+    hx_ref, replaced, mask_ref, v1_ref, p_ref, stage, along_z, along_y,
 ):
     x = pl.program_id(0)
 
     @pl.when(x == 0)
     def _():
-        weno_terms(sums, kr_ref, across, terms_out)
         hx_ref[...] = jnp.zeros((256, CZ), BF16)
         mask_ref[...] = jnp.zeros((ROWS, 128), F32)
         flat = replaced.reshape(2, VARIABLES * ROWS, 128)
-        packed = terms_out.reshape(2, VARIABLES * PENCILS, 128)
+        packed = terms_ref.reshape(2, VARIABLES * PENCILS, 128)
 
         def scatter(p, carry):
             row = list_ref[p]
@@ -480,7 +483,7 @@
         advance_body,
         grid=(CX,),
         out_shape=jax.ShapeDtypeStruct((VARIABLES, CX, CY, CZ), F32),
-        in_specs=[SMEM, SMEM] + [VMEM] * 7,
+        in_specs=[SMEM, SMEM] + [VMEM] * 6,
         out_specs=pl.BlockSpec((VARIABLES, 1, CY, CZ), lambda x: (0, x, 0, 0)),
         scratch_shapes=[
             pltpu.VMEM((256, CZ), BF16),
@@ -491,8 +494,6 @@
             pltpu.VMEM((VARIABLES, CY, 512), BF16),
             pltpu.VMEM((VARIABLES, CY, CZ), F32),
             pltpu.VMEM((2, 2, 80, 128), F32),
-            pltpu.VMEM((VARIABLES, CZ, 128), F32),
-            pltpu.VMEM((2, VARIABLES, PENCILS, 128), F32),
         ],
         compiler_params=pltpu.CompilerParams(vmem_limit_bytes=36 << 20),
         name="advance",

time: 33.6 us -> 31.2 us (0.929)
  the two profiles are of different devices: /device:TPU:30 before, /device:TPU:13 now
where the time goes in v1:
time: 31.2 us; the launch traced here: 30.8 us
  Pallas kernels  30 us (96%)
  between operations  0.72 us (2%)
    pallas_call x1, Pallas kernels, prepare(): pl.pallas_call(prepare_body, out_shape=(pltpu.VMEM((2, VARIABLES, CX, CY,...  18.7 us
    pallas_call x1, Pallas kernels, advance(): pl.pallas_call(advance_body, grid=(CX,), out_shape=jax.ShapeDtypeStruct((...  11.3 us

profile of v1, /device:TPU:13, one launch (start us, length us, event | category | flops | bytes accessed | tf_op | source)
XLA Modules:
  0.0 30.8 jit_solution(16234270681644726240)
XLA Ops:
  0.0 0.0 copy-start.1
  0.0 0.0 copy-start
  0.0 0.0 copy-start.2
  0.7 18.7 %prepare.1 = (f32[2,14,8,64,128]{4,3,2,1,0:T(8,128)S(1)}, f32[2,14,128,128]{3,2,1,0:T(8,128)S(1)}, f32[2,2,14,24,128]{4,3,2,1,0:T(8,128)S(1)}, bf16[14,64,256]{2,1,0:T(8,128)(2,1)S(1)}) custom-call(s32[128]{0:T(128)} %bitcast.2, s32[1,128]{1,0:T(1,128)} %bitcast.3, f32[14,14]{1,0:T(8,128)} %left_ref.1, f32[14,14]{1,0:T(8,128)} %right_ref.1, ...), custom_call_target="tpu_custom_call" | custom-call | tf_op jit(solution)/shard_map/prepare/pallas_call | solution.py:367
  19.4 0.0 copy-done.1
  19.4 0.0 copy-done
  19.4 0.0 copy-done.2
  19.4 11.3 %advance.1 = f32[14,8,64,256]{3,2,1,0:T(8,128)} custom-call(s32[128]{0:T(128)S(1)} %bitcast.4, s32[1,1,1]{2,1,0:T(1,128)S(6)} %copy.8.count_ref, f32[2,14,8,64,128]{4,3,2,1,0:T(8,128)S(1)} %get-tuple-element.9.u_ref, f32[2,14,128,128]{3,2,1,0:T(8,128)S(1)} %get-tuple-element.10.terms_ref, f32[2,2,14,24,128]{4,3,2,1,0:T(8,128)S(1)} %get-tuple-element.11.yflux, ...), custom_call_target="tpu_custom_call" | custom-call | tf_op jit(solution)/shard_map/advance/pallas_call | solution.py:482
Async XLA Ops:
  0.0 19.4 %copy-start.1 = (bf16[16,256]{1,0:T(8,128)(2,1)S(1)}, bf16[16,256]{1,0:T(8,128)(2,1)}, u32[]{:S(2)}) copy-start(bf16[16,256]{1,0:T(8,128)(2,1)} %constant.5.clone.hcoef_ref) | copy-start | bytes 24580
  0.0 19.4 %copy-start = (bf16[256,256]{1,0:T(8,128)(2,1)S(1)}, bf16[256,256]{1,0:T(8,128)(2,1)}, u32[]{:S(2)}) copy-start(bf16[256,256]{1,0:T(8,128)(2,1)} %constant.4.clone.zcoef_ref) | copy-start | bytes 393220
  0.0 19.4 %copy-start.2 = (s32[1,1,1,128]{3,2,1,0:T(1,128)S(1)}, s32[1,1,1,128]{3,2,1,0:T(1,128)}, u32[]{:S(2)}) copy-start(s32[1,1,1,128]{3,2,1,0:T(1,128)} %param.10) | copy-start | bytes 1540

commit v2 on v1

--- a/solution.py
+++ b/solution.py
@@ -169,14 +169,14 @@
             across[:, rows, :] = result[:, 128 * k : 128 * k + 128].reshape(VARIABLES, 16, 128)
         return carry
 
-    lax.fori_loop(0, CZ // 32, chunk, 0, unroll=4)
+    lax.fori_loop(0, CZ // 32, chunk, 0, unroll=8)
 
     def turn_back(v, carry):
         for t in range(2):
             terms_out[t, v] = across[v, 128 * t : 128 * t + 128, :].T
         return carry
 
-    lax.fori_loop(0, VARIABLES, turn_back, 0, unroll=2)
+    lax.fori_loop(0, VARIABLES, turn_back, 0, unroll=7)
 
 
 def prepare_body(
@@ -303,7 +303,7 @@
         pressure_ref[rows, :] = pressure
         return jnp.maximum(peak, jnp.abs(velocity))
 
-    peak = lax.fori_loop(1, 33, wave, jnp.zeros((8, 128), F32), unroll=2)
+    peak = lax.fori_loop(1, 33, wave, jnp.zeros((8, 128), F32), unroll=4)
 
     def chunk(i, carry):
         first = pl.ds(pl.multiple_of(32 * i + 8, 8), 16)
@@ -314,7 +314,7 @@
         proj[:, second, :] = result[:, 128:256].reshape(VARIABLES, 16, 128)
         return carry
 
-    lax.fori_loop(0, CZ // 32, chunk, 0, unroll=4)
+    lax.fori_loop(0, CZ // 32, chunk, 0, unroll=8)
 
     ends.wait()
     own_y = jnp.broadcast_to(where_ref[...] % CY, (2 * CY, PENCILS))

time: 31.2 us -> 30.4 us (0.974)
  the two profiles are of different devices: /device:TPU:13 before, /device:TPU:26 now
where the time goes in v2:
time: 30.4 us; the launch traced here: 30.2 us
  Pallas kernels  29.5 us (97%)
  between operations  0.72 us (2%)
    pallas_call x1, Pallas kernels, prepare(): pl.pallas_call(prepare_body, out_shape=(pltpu.VMEM((2, VARIABLES, CX, CY,...  18.1 us
    pallas_call x1, Pallas kernels, advance(): pl.pallas_call(advance_body, grid=(CX,), out_shape=jax.ShapeDtypeStruct((...  11.3 us

profile of v2, /device:TPU:26, one launch (start us, length us, event | category | flops | bytes accessed | tf_op | source)
XLA Modules:
  0.0 30.2 jit_solution(17317797905304380612)
XLA Ops:
  0.0 0.0 copy-start.1
  0.0 0.0 copy-start
  0.0 0.0 copy-start.2
  0.7 18.1 %prepare.1 = (f32[2,14,8,64,128]{4,3,2,1,0:T(8,128)S(1)}, f32[2,14,128,128]{3,2,1,0:T(8,128)S(1)}, f32[2,2,14,24,128]{4,3,2,1,0:T(8,128)S(1)}, bf16[14,64,256]{2,1,0:T(8,128)(2,1)S(1)}) custom-call(s32[128]{0:T(128)} %bitcast.2, s32[1,128]{1,0:T(1,128)} %bitcast.3, f32[14,14]{1,0:T(8,128)} %left_ref.1, f32[14,14]{1,0:T(8,128)} %right_ref.1, ...), custom_call_target="tpu_custom_call" | custom-call | tf_op jit(solution)/shard_map/prepare/pallas_call | solution.py:367
  18.8 0.0 copy-done.1
  18.8 0.0 copy-done
  18.9 0.0 copy-done.2
  18.9 11.3 %advance.1 = f32[14,8,64,256]{3,2,1,0:T(8,128)} custom-call(s32[128]{0:T(128)S(1)} %bitcast.4, s32[1,1,1]{2,1,0:T(1,128)S(6)} %copy.8.count_ref, f32[2,14,8,64,128]{4,3,2,1,0:T(8,128)S(1)} %get-tuple-element.9.u_ref, f32[2,14,128,128]{3,2,1,0:T(8,128)S(1)} %get-tuple-element.10.terms_ref, f32[2,2,14,24,128]{4,3,2,1,0:T(8,128)S(1)} %get-tuple-element.11.yflux, ...), custom_call_target="tpu_custom_call" | custom-call | tf_op jit(solution)/shard_map/advance/pallas_call | solution.py:482
Async XLA Ops:
  0.0 18.8 %copy-start.1 = (bf16[16,256]{1,0:T(8,128)(2,1)S(1)}, bf16[16,256]{1,0:T(8,128)(2,1)}, u32[]{:S(2)}) copy-start(bf16[16,256]{1,0:T(8,128)(2,1)} %constant.5.clone.hcoef_ref) | copy-start | bytes 24580
  0.0 18.8 %copy-start = (bf16[256,256]{1,0:T(8,128)(2,1)S(1)}, bf16[256,256]{1,0:T(8,128)(2,1)}, u32[]{:S(2)}) copy-start(bf16[256,256]{1,0:T(8,128)(2,1)} %constant.4.clone.zcoef_ref) | copy-start | bytes 393220
  0.0 18.9 %copy-start.2 = (s32[1,1,1,128]{3,2,1,0:T(1,128)S(1)}, s32[1,1,1,128]{3,2,1,0:T(1,128)}, u32[]{:S(2)}) copy-start(s32[1,1,1,128]{3,2,1,0:T(1,128)} %param.10) | copy-start | bytes 1540
